TPU v7x, 32 devices: a whole 2x2x4 slice. The times are simulated.
32 devices in a mesh: gy: 4 (over y, core), gx: 8 (over z, x).
Axes of the slice: x: 2, y: 2, z: 4, core: 2. Of those that a mesh axis runs over, the one named last changes fastest.
Arguments:
- phase: float32 [2, 128, 1024], P(None, 'gy', 'gx'), may hold values from -1.5 to 1.5
- velocity: float32 [2, 128, 1024], P(None, 'gy', 'gx'), may hold values from -2 to 2
- offsets: int32 [2, 4], replicated, may hold values from 0 to 1020, as said below
Outputs:
- phase_out: float32 [2, 128, 1024], P(None, 'gy', 'gx')
Inputs may be any that keep to these rules, and one draw needn't show every extreme that they name: `offsets`: every offset is a multiple of 2 ** 2.
All inputs are finite; a program needn't handle non-finite values.
Results may differ from a plain program's by a relative error of at most 0.00014.
Values sent between devices are 32-bit elements; how exact they have to be, the bound alone decides.
No kernel may reach another device: no remote copies, remote signals or barrier semaphores. Data moves between devices by JAX's collectives and lax.ppermute only.
A program may use at most 64 MiB of HBM per device.

v0:
```python
import jax
import jax.numpy as jnp
from jax import lax
from jax.sharding import PartitionSpec as P

STEPS = 2
ITERS = 2
LEVELS = 3
COARSE = 4
RELAXATION = 0.8
DIFFUSION = 4.0
VERTICAL = 1.0
REACTION = 0.5
ADVECTION = 0.5


def padded(cells, sides, width):
    for axis, dim in sides:
        count = lax.axis_size(axis)
        head = lax.slice_in_dim(cells, 0, width, axis=dim)
        tail = lax.slice_in_dim(cells, cells.shape[dim] - width, cells.shape[dim], axis=dim)
        cells = jnp.concatenate(
            [
                lax.ppermute(tail, axis, [(i, (i + 1) % count) for i in range(count)]),
                cells,
                lax.ppermute(head, axis, [((i + 1) % count, i) for i in range(count)]),
            ],
            axis=dim,
        )
    return cells


def sheared(bottom_row, upper_row, offsets_now, anchor, columns):
    breadth = bottom_row.shape[1]
    device_row = lax.axis_index("gy")
    row_count = lax.axis_size("gy")
    below_shift = offsets_now[device_row]
    above_shift = offsets_now[(device_row + 1) % row_count]
    local_columns = jnp.arange(columns, dtype=jnp.int32)
    down_index = (anchor + below_shift + local_columns) % breadth
    up_index = (anchor - above_shift + local_columns) % breadth
    down_window = jnp.take(bottom_row, down_index, axis=1)
    up_window = jnp.take(upper_row, up_index, axis=1)
    stacked = jnp.stack([down_window, up_window], axis=1)
    rims = padded(stacked, (("gy", 1),), 1)
    return (rims[:, 0, :], rims[:, 3, :])


def stencil(field, below_row, above_row, across, coupling):
    diagonal = 1.0 + 4.0 * coupling + 2.0 * VERTICAL
    column_pad = jnp.concatenate([below_row[:, None, :], field, above_row[:, None, :]], axis=1)
    beside = column_pad[:, 2:, :] + column_pad[:, :-2, :] + across
    vertical_sum = jnp.roll(field, 1, 0) + jnp.roll(field, -1, 0)
    return diagonal * field - coupling * beside - VERTICAL * vertical_sum


def operate(field, offsets_now, coupling):
    columns = field.shape[2]
    margins = padded(field, (("gx", 2),), 1)
    bottom_full, upper_full = (
        lax.all_gather(field[:, 0, :], "gx", axis=1, tiled=True),
        lax.all_gather(field[:, -1, :], "gx", axis=1, tiled=True),
    )
    right_field = margins[:, :, 2:]
    left_field = margins[:, :, :-2]
    below_row, above_row = sheared(
        bottom_full, upper_full, offsets_now, lax.axis_index("gx") * columns, columns
    )
    across = right_field + left_field
    return (stencil(field, below_row, above_row, across, coupling), right_field, left_field)


def operate_strip(field, offsets_now, coupling):
    below_row, above_row = sheared(field[:, 0, :], field[:, -1, :], offsets_now, 0, field.shape[2])
    across = jnp.roll(field, 1, 2) + jnp.roll(field, -1, 2)
    return stencil(field, below_row, above_row, across, coupling)


def coarsest(residual, offsets_now, coupling):
    diagonal = 1.0 + 4.0 * coupling + 2.0 * VERTICAL
    columns = residual.shape[2]
    gathered = lax.all_gather(residual, "gx", axis=2, tiled=True)
    estimate = RELAXATION * gathered / diagonal
    for sweep_index in range(COARSE - 1):
        estimate = (
            estimate
            + RELAXATION * (gathered - operate_strip(estimate, offsets_now, coupling)) / diagonal
        )
    return lax.dynamic_slice_in_dim(estimate, lax.axis_index("gx") * columns, columns, 2)


def vcycle(residual, offsets_raw, layer_index):
    factor = 2**layer_index
    coupling = DIFFUSION / 4.0**layer_index
    diagonal = 1.0 + 4.0 * coupling + 2.0 * VERTICAL
    offsets_now = offsets_raw // factor
    if layer_index == LEVELS - 1:
        return coarsest(residual, offsets_now, coupling)
    estimate = RELAXATION * residual / diagonal
    defect = residual - operate(estimate, offsets_now, coupling)[0]
    planes, height, breadth = defect.shape
    coarser = defect.reshape(planes, height // 2, 2, breadth // 2, 2).mean(axis=(2, 4))
    correction = vcycle(coarser, offsets_raw, layer_index + 1)
    estimate = estimate + jnp.repeat(jnp.repeat(correction, 2, axis=1), 2, axis=2)
    estimate = (
        estimate + RELAXATION * (residual - operate(estimate, offsets_now, coupling)[0]) / diagonal
    )
    return estimate


def total_inner(first_field, second_field):
    return lax.psum(jnp.sum(first_field * second_field), ("gy", "gx"))


def local(phase, velocity, offsets):
    phase_now = phase
    for time_step in range(STEPS):
        offsets_raw = offsets[time_step]
        applied, right_field, left_field = operate(phase_now, offsets_raw, DIFFUSION)
        source = (
            phase_now
            + REACTION * (phase_now - phase_now * phase_now * phase_now)
            - ADVECTION * velocity * (right_field - left_field)
        )
        residual = source - applied
        precond = vcycle(residual, offsets_raw, 0)
        projected = total_inner(residual, precond)
        direction = precond
        for iteration in range(ITERS):
            image = operate(direction, offsets_raw, DIFFUSION)[0]
            step_size = projected / total_inner(direction, image)
            phase_now = phase_now + step_size * direction
            residual = residual - step_size * image
            if iteration + 1 < ITERS:
                precond = vcycle(residual, offsets_raw, 0)
                following = total_inner(residual, precond)
                direction = precond + following / projected * direction
                projected = following
    return phase_now


def solution(mesh):
    placed = (P(None, "gy", "gx"), P(None, "gy", "gx"), P())
    return jax.shard_map(
        local, mesh=mesh, in_specs=placed, out_specs=P(None, "gy", "gx"), check_vma=False
    )
```

profile of v0, /device:TPU:12, one launch (start us, length us, event | category | flops | bytes accessed | tf_op | source)
XLA Modules:
  0.0 1669.2 jit_solution(4805464784161272798)
XLA Ops:
  6.4 31.0 %all-gather.1 = f32[2,1,1024]{0,2,1:T(8,128)S(1)} all-gather(f32[2,1,128]{0,2,1:T(8,128)S(1)} %copy.2969), channel_id=3, replica_groups=mesh['gy'=4,'gx'=8] {'gx'}, dimensions={2}, use_global_device_ids=true | all-gather | bytes 9216 | tf_op jit(solution)/shard_map/all_gather | solution.py:62
  38.3 31.4 %all-gather = f32[2,1,1024]{0,2,1:T(8,128)S(1)} all-gather(f32[2,1,128]{0,2,1:T(8,128)S(1)} %copy.2968), channel_id=2, replica_groups=mesh['gy'=4,'gx'=8] {'gx'}, dimensions={2}, use_global_device_ids=true | all-gather | bytes 9216 | tf_op jit(solution)/shard_map/all_gather | solution.py:61
  83.4 20.7 %all-gather.2 = f32[2,1,1024]{2,1,0:T(1,128)S(1)} all-gather(f32[2,1,128]{2,1,0:T(1,128)S(1)} %get-tuple-element.104), channel_id=4, replica_groups=mesh['gy'=4,'gx'=8] {'gx'}, dimensions={2}, use_global_device_ids=true | all-gather | bytes 9216 | tf_op jit(solution)/shard_map/all_gather | solution.py:61
  135.9 29.8 %all-gather.5 = f32[2,1,512]{0,1,2:T(1,128)S(1)} all-gather(f32[2,1,64]{0,1,2:T(1,128)S(1)} %copy.2705), channel_id=7, replica_groups=mesh['gy'=4,'gx'=8] {'gx'}, dimensions={2}, use_global_device_ids=true | all-gather | bytes 4608 | tf_op jit(solution)/shard_map/all_gather | solution.py:62
  166.5 30.8 %all-gather.4 = f32[2,1,512]{0,1,2:T(1,128)S(1)} all-gather(f32[2,1,64]{0,1,2:T(1,128)S(1)} %copy.2702), channel_id=6, replica_groups=mesh['gy'=4,'gx'=8] {'gx'}, dimensions={2}, use_global_device_ids=true | all-gather | bytes 4608 | tf_op jit(solution)/shard_map/all_gather | solution.py:61
  200.2 30.9 %all_gather.150 = f32[2,8,256]{1,0,2:T(2,128)S(1)} all-gather(f32[2,8,32]{1,0,2:T(2,128)S(1)} %copy.2708), channel_id=1, replica_groups=mesh['gy'=4,'gx'=8] {'gx'}, dimensions={2}, use_global_device_ids=true | all-gather | bytes 18432 | tf_op jit(solution)/shard_map/all_gather | solution.py:82
  252.2 30.9 %all-gather.7 = f32[2,1,512]{0,1,2:T(1,128)S(1)} all-gather(f32[2,1,64]{0,1,2:T(1,128)S(1)} %copy.2731), channel_id=9, replica_groups=mesh['gy'=4,'gx'=8] {'gx'}, dimensions={2}, use_global_device_ids=true | all-gather | bytes 4608 | tf_op jit(solution)/shard_map/all_gather | solution.py:62
  283.9 30.9 %all-gather.6 = f32[2,1,512]{0,1,2:T(1,128)S(1)} all-gather(f32[2,1,64]{0,1,2:T(1,128)S(1)} %copy.2728), channel_id=8, replica_groups=mesh['gy'=4,'gx'=8] {'gx'}, dimensions={2}, use_global_device_ids=true | all-gather | bytes 4608 | tf_op jit(solution)/shard_map/all_gather | solution.py:61
  409.6 42.1 %all-reduce.1 = (f32[]{:T(128)}, f32[]{:T(128)}) all-reduce(f32[]{:T(128)} %get-tuple-element.11, f32[]{:T(128)} %get-tuple-element.10), channel_id=1, replica_groups=mesh['gy'=4,'gx'=8] {'gy','gx'}, use_global_device_ids=true, to_apply=%region_3.7 | all-reduce | flops 2 | bytes 16 | tf_op jit(solution)/shard_map/psum | solution.py:112
  499.5 29.8 %all-gather.15 = f32[2,1,512]{0,1,2:T(1,128)S(1)} all-gather(f32[2,1,64]{0,1,2:T(1,128)S(1)} %copy.2751), channel_id=17, replica_groups=mesh['gy'=4,'gx'=8] {'gx'}, dimensions={2}, use_global_device_ids=true | all-gather | bytes 4608 | tf_op jit(solution)/shard_map/all_gather | solution.py:62
  530.1 30.7 %all-gather.14 = f32[2,1,512]{0,1,2:T(1,128)S(1)} all-gather(f32[2,1,64]{0,1,2:T(1,128)S(1)} %copy.2748), channel_id=16, replica_groups=mesh['gy'=4,'gx'=8] {'gx'}, dimensions={2}, use_global_device_ids=true | all-gather | bytes 4608 | tf_op jit(solution)/shard_map/all_gather | solution.py:61
  563.8 30.8 %all_gather.161 = f32[2,8,256]{1,0,2:T(2,128)S(1)} all-gather(f32[2,8,32]{1,0,2:T(2,128)S(1)} %copy.2754), channel_id=1, replica_groups=mesh['gy'=4,'gx'=8] {'gx'}, dimensions={2}, use_global_device_ids=true | all-gather | bytes 18432 | tf_op jit(solution)/shard_map/all_gather | solution.py:82
  616.1 30.9 %all-gather.17 = f32[2,1,512]{0,1,2:T(1,128)S(1)} all-gather(f32[2,1,64]{0,1,2:T(1,128)S(1)} %copy.2777), channel_id=19, replica_groups=mesh['gy'=4,'gx'=8] {'gx'}, dimensions={2}, use_global_device_ids=true | all-gather | bytes 4608 | tf_op jit(solution)/shard_map/all_gather | solution.py:62
  647.8 30.8 %all-gather.16 = f32[2,1,512]{0,1,2:T(1,128)S(1)} all-gather(f32[2,1,64]{0,1,2:T(1,128)S(1)} %copy.2774), channel_id=18, replica_groups=mesh['gy'=4,'gx'=8] {'gx'}, dimensions={2}, use_global_device_ids=true | all-gather | bytes 4608 | tf_op jit(solution)/shard_map/all_gather | solution.py:61
  681.1 20.7 %all-gather.18 = f32[2,1,1024]{2,1,0:T(1,128)S(1)} all-gather(f32[2,1,128]{2,1,0:T(1,128)S(1)} %get-tuple-element.78), channel_id=20, replica_groups=mesh['gy'=4,'gx'=8] {'gx'}, dimensions={2}, use_global_device_ids=true | all-gather | bytes 9216 | tf_op jit(solution)/shard_map/all_gather | solution.py:61
  728.5 42.0 %psum.58 = f32[]{:T(128)} all-reduce(f32[]{:T(128)} %get-tuple-element.23), channel_id=1, replica_groups=mesh['gy'=4,'gx'=8] {'gy','gx'}, use_global_device_ids=true, to_apply=%region_9.13 | all-reduce | flops 1 | bytes 8 | tf_op jit(solution)/shard_map/psum | solution.py:112
  813.3 42.1 %psum.59 = f32[]{:T(128)} all-reduce(f32[]{:T(128)} %fusion.65), channel_id=1, replica_groups=mesh['gy'=4,'gx'=8] {'gy','gx'}, use_global_device_ids=true, to_apply=%region_11.15 | all-reduce | flops 1 | bytes 8 | tf_op jit(solution)/shard_map/psum | solution.py:112
  948.0 29.8 %all-gather.27 = f32[2,1,512]{0,1,2:T(1,128)S(1)} all-gather(f32[2,1,64]{0,1,2:T(1,128)S(1)} %copy.2801), channel_id=29, replica_groups=mesh['gy'=4,'gx'=8] {'gx'}, dimensions={2}, use_global_device_ids=true | all-gather | bytes 4608 | tf_op jit(solution)/shard_map/all_gather | solution.py:62
  978.6 30.8 %all-gather.26 = f32[2,1,512]{0,1,2:T(1,128)S(1)} all-gather(f32[2,1,64]{0,1,2:T(1,128)S(1)} %copy.2798), channel_id=28, replica_groups=mesh['gy'=4,'gx'=8] {'gx'}, dimensions={2}, use_global_device_ids=true | all-gather | bytes 4608 | tf_op jit(solution)/shard_map/all_gather | solution.py:61
  1012.3 30.9 %all_gather.174 = f32[2,8,256]{1,0,2:T(2,128)S(1)} all-gather(f32[2,8,32]{1,0,2:T(2,128)S(1)} %copy.2804), channel_id=1, replica_groups=mesh['gy'=4,'gx'=8] {'gx'}, dimensions={2}, use_global_device_ids=true | all-gather | bytes 18432 | tf_op jit(solution)/shard_map/all_gather | solution.py:82
  1064.4 30.9 %all-gather.29 = f32[2,1,512]{0,1,2:T(1,128)S(1)} all-gather(f32[2,1,64]{0,1,2:T(1,128)S(1)} %copy.2827), channel_id=31, replica_groups=mesh['gy'=4,'gx'=8] {'gx'}, dimensions={2}, use_global_device_ids=true | all-gather | bytes 4608 | tf_op jit(solution)/shard_map/all_gather | solution.py:62
  1096.0 30.8 %all-gather.28 = f32[2,1,512]{0,1,2:T(1,128)S(1)} all-gather(f32[2,1,64]{0,1,2:T(1,128)S(1)} %copy.2824), channel_id=30, replica_groups=mesh['gy'=4,'gx'=8] {'gx'}, dimensions={2}, use_global_device_ids=true | all-gather | bytes 4608 | tf_op jit(solution)/shard_map/all_gather | solution.py:61
  1129.3 20.7 %all-gather.30 = f32[2,1,1024]{2,1,0:T(1,128)S(1)} all-gather(f32[2,1,128]{2,1,0:T(1,128)S(1)} %get-tuple-element.56), channel_id=32, replica_groups=mesh['gy'=4,'gx'=8] {'gx'}, dimensions={2}, use_global_device_ids=true | all-gather | bytes 9216 | tf_op jit(solution)/shard_map/all_gather | solution.py:61
  1221.2 42.3 %all-reduce = (f32[]{:T(128)}, f32[]{:T(128)}) all-reduce(f32[]{:T(128)} %get-tuple-element.8, f32[]{:T(128)} %get-tuple-element.6), channel_id=1, replica_groups=mesh['gy'=4,'gx'=8] {'gy','gx'}, use_global_device_ids=true, to_apply=%region_15.19 | all-reduce | flops 2 | bytes 16 | tf_op jit(solution)/shard_map/psum | solution.py:112
  1311.4 29.9 %all-gather.37 = f32[2,1,512]{0,1,2:T(1,128)S(1)} all-gather(f32[2,1,64]{0,1,2:T(1,128)S(1)} %copy.2847), channel_id=39, replica_groups=mesh['gy'=4,'gx'=8] {'gx'}, dimensions={2}, use_global_device_ids=true | all-gather | bytes 4608 | tf_op jit(solution)/shard_map/all_gather | solution.py:62
  1342.0 30.7 %all-gather.36 = f32[2,1,512]{0,1,2:T(1,128)S(1)} all-gather(f32[2,1,64]{0,1,2:T(1,128)S(1)} %copy.2844), channel_id=38, replica_groups=mesh['gy'=4,'gx'=8] {'gx'}, dimensions={2}, use_global_device_ids=true | all-gather | bytes 4608 | tf_op jit(solution)/shard_map/all_gather | solution.py:61
  1375.7 30.8 %all_gather.185 = f32[2,8,256]{1,0,2:T(2,128)S(1)} all-gather(f32[2,8,32]{1,0,2:T(2,128)S(1)} %copy.2850), channel_id=1, replica_groups=mesh['gy'=4,'gx'=8] {'gx'}, dimensions={2}, use_global_device_ids=true | all-gather | bytes 18432 | tf_op jit(solution)/shard_map/all_gather | solution.py:82
  1427.8 30.8 %all-gather.39 = f32[2,1,512]{0,1,2:T(1,128)S(1)} all-gather(f32[2,1,64]{0,1,2:T(1,128)S(1)} %copy.2873), channel_id=41, replica_groups=mesh['gy'=4,'gx'=8] {'gx'}, dimensions={2}, use_global_device_ids=true | all-gather | bytes 4608 | tf_op jit(solution)/shard_map/all_gather | solution.py:62
  1459.3 31.0 %all-gather.38 = f32[2,1,512]{0,1,2:T(1,128)S(1)} all-gather(f32[2,1,64]{0,1,2:T(1,128)S(1)} %copy.2870), channel_id=40, replica_groups=mesh['gy'=4,'gx'=8] {'gx'}, dimensions={2}, use_global_device_ids=true | all-gather | bytes 4608 | tf_op jit(solution)/shard_map/all_gather | solution.py:61
  1492.8 21.0 %all-gather.40 = f32[2,1,1024]{2,1,0:T(1,128)S(1)} all-gather(f32[2,1,128]{2,1,0:T(1,128)S(1)} %get-tuple-element.36), channel_id=42, replica_groups=mesh['gy'=4,'gx'=8] {'gx'}, dimensions={2}, use_global_device_ids=true | all-gather | bytes 9216 | tf_op jit(solution)/shard_map/all_gather | solution.py:61
  1540.5 41.9 %psum.62 = f32[]{:T(128)} all-reduce(f32[]{:T(128)} %get-tuple-element.16), channel_id=1, replica_groups=mesh['gy'=4,'gx'=8] {'gy','gx'}, use_global_device_ids=true, to_apply=%region_21.25 | all-reduce | flops 1 | bytes 8 | tf_op jit(solution)/shard_map/psum | solution.py:112
  1625.2 41.9 %psum.63 = f32[]{:T(128)} all-reduce(f32[]{:T(128)} %fusion.14), channel_id=1, replica_groups=mesh['gy'=4,'gx'=8] {'gy','gx'}, use_global_device_ids=true, to_apply=%region_23.27 | all-reduce | flops 1 | bytes 8 | tf_op jit(solution)/shard_map/psum | solution.py:112
  (817 shorter events, 642.1 us)
Async XLA Ops:
  0.9 81.3 %collective-permute-start = (f32[2,32,1]{2,1,0:T(8,128)S(1)}, f32[2,32,1]{2,1,0:T(8,128)S(1)}, u32[]{:S(2)}, u32[]{:S(2)}) collective-permute-start(f32[2,32,1]{2,1,0:T(8,128)S(1)} %get-tuple-element.108), channel_id=1, source_target_pairs={{1,0},{2,1},{3,2},{4,3},{5,4},{6,5},{7,6},{0,7},{9,8},{10,9},{11,1... | collective-permute-start | bytes 776 | tf_op jit(solution)/shard_map/ppermute | solution.py:26
  2.3 80.0 %collective-permute-start.1 = (f32[2,32,1]{2,1,0:T(8,128)S(1)}, f32[2,32,1]{2,1,0:T(8,128)S(1)}, u32[]{:S(2)}, u32[]{:S(2)}) collective-permute-start(f32[2,32,1]{2,1,0:T(8,128)S(1)} %get-tuple-element.109), channel_id=1, source_target_pairs={{0,1},{1,2},{2,3},{3,4},{4,5},{5,6},{6,7},{7,0},{8,9},{9,10},{10,1... | collective-permute-start | bytes 776 | tf_op jit(solution)/shard_map/ppermute | solution.py:24
  38.1 44.2 %collective-permute-start.3 = (f32[2,1,128]{2,1,0:T(1,128)S(1)}, f32[2,1,128]{2,1,0:T(1,128)S(1)}, u32[]{:S(2)}, u32[]{:S(2)}) collective-permute-start(f32[2,1,128]{2,1,0:T(1,128)S(1)} %bitcast.402), channel_id=1, source_target_pairs={{0,8},{8,16},{16,24},{24,0},{1,9},{9,17},{17,25},{25,1},{2,10},{10... | collective-permute-start | bytes 3080 | tf_op jit(solution)/shard_map/ppermute | solution.py:24
  70.4 11.9 collective-permute-start.2
  120.4 8.4 collective-permute-start.6
  133.0 65.1 %collective-permute-start.10 = (f32[2,16,1]{2,1,0:T(8,128)S(1)}, f32[2,16,1]{2,1,0:T(8,128)S(1)}, u32[]{:S(2)}, u32[]{:S(2)}) collective-permute-start(f32[2,16,1]{2,1,0:T(8,128)S(1)} %get-tuple-element.256), channel_id=1, source_target_pairs={{1,0},{2,1},{3,2},{4,3},{5,4},{6,5},{7,6},{0,7},{9,8},{10,9},{11,1... | collective-permute-start | bytes 392 | tf_op jit(solution)/shard_map/ppermute | solution.py:26
  135.9 62.1 %collective-permute-start.11 = (f32[2,16,1]{2,1,0:T(8,128)S(1)}, f32[2,16,1]{2,1,0:T(8,128)S(1)}, u32[]{:S(2)}, u32[]{:S(2)}) collective-permute-start(f32[2,16,1]{2,1,0:T(8,128)S(1)} %get-tuple-element.257), channel_id=1, source_target_pairs={{0,1},{1,2},{2,3},{3,4},{4,5},{5,6},{6,7},{7,0},{8,9},{9,10},{10,1... | collective-permute-start | bytes 392 | tf_op jit(solution)/shard_map/ppermute | solution.py:24
  166.5 31.6 %collective-permute-start.9 = (f32[2,1,64]{2,1,0:T(1,128)S(1)}, f32[2,1,64]{2,1,0:T(1,128)S(1)}, u32[]{:S(2)}, u32[]{:S(2)}) collective-permute-start(f32[2,1,64]{2,1,0:T(1,128)S(1)} %copy.2707), channel_id=1, source_target_pairs={{0,8},{8,16},{16,24},{24,0},{1,9},{9,17},{17,25},{25,1},{2,10},{10... | collective-permute-start | bytes 1544 | tf_op jit(solution)/shard_map/ppermute | solution.py:24
  247.6 67.9 %collective-permute-start.20 = (f32[2,16,1]{2,1,0:T(8,128)S(1)}, f32[2,16,1]{2,1,0:T(8,128)S(1)}, u32[]{:S(2)}, u32[]{:S(2)}) collective-permute-start(f32[2,16,1]{2,1,0:T(8,128)S(1)} %get-tuple-element.226), channel_id=1, source_target_pairs={{1,0},{2,1},{3,2},{4,3},{5,4},{6,5},{7,6},{0,7},{9,8},{10,9},{11,1... | collective-permute-start | bytes 392 | tf_op jit(solution)/shard_map/ppermute | solution.py:26
  252.2 63.3 %collective-permute-start.21 = (f32[2,16,1]{2,1,0:T(8,128)S(1)}, f32[2,16,1]{2,1,0:T(8,128)S(1)}, u32[]{:S(2)}, u32[]{:S(2)}) collective-permute-start(f32[2,16,1]{2,1,0:T(8,128)S(1)} %get-tuple-element.227), channel_id=1, source_target_pairs={{0,1},{1,2},{2,3},{3,4},{4,5},{5,6},{6,7},{7,0},{8,9},{9,10},{10,1... | collective-permute-start | bytes 392 | tf_op jit(solution)/shard_map/ppermute | solution.py:24
  283.9 31.7 %collective-permute-start.19 = (f32[2,1,64]{2,1,0:T(1,128)S(1)}, f32[2,1,64]{2,1,0:T(1,128)S(1)}, u32[]{:S(2)}, u32[]{:S(2)}) collective-permute-start(f32[2,1,64]{2,1,0:T(1,128)S(1)} %copy.2733), channel_id=1, source_target_pairs={{0,8},{8,16},{16,24},{24,0},{1,9},{9,17},{17,25},{25,1},{2,10},{10... | collective-permute-start | bytes 1544 | tf_op jit(solution)/shard_map/ppermute | solution.py:24
  398.7 8.9 collective-permute-start.28
  496.6 65.0 %collective-permute-start.36 = (f32[2,16,1]{2,1,0:T(8,128)S(1)}, f32[2,16,1]{2,1,0:T(8,128)S(1)}, u32[]{:S(2)}, u32[]{:S(2)}) collective-permute-start(f32[2,16,1]{2,1,0:T(8,128)S(1)} %get-tuple-element.220), channel_id=1, source_target_pairs={{1,0},{2,1},{3,2},{4,3},{5,4},{6,5},{7,6},{0,7},{9,8},{10,9},{11,1... | collective-permute-start | bytes 392 | tf_op jit(solution)/shard_map/ppermute | solution.py:26
  499.5 62.1 %collective-permute-start.37 = (f32[2,16,1]{2,1,0:T(8,128)S(1)}, f32[2,16,1]{2,1,0:T(8,128)S(1)}, u32[]{:S(2)}, u32[]{:S(2)}) collective-permute-start(f32[2,16,1]{2,1,0:T(8,128)S(1)} %get-tuple-element.221), channel_id=1, source_target_pairs={{0,1},{1,2},{2,3},{3,4},{4,5},{5,6},{6,7},{7,0},{8,9},{9,10},{10,1... | collective-permute-start | bytes 392 | tf_op jit(solution)/shard_map/ppermute | solution.py:24
  530.1 31.5 %collective-permute-start.35 = (f32[2,1,64]{2,1,0:T(1,128)S(1)}, f32[2,1,64]{2,1,0:T(1,128)S(1)}, u32[]{:S(2)}, u32[]{:S(2)}) collective-permute-start(f32[2,1,64]{2,1,0:T(1,128)S(1)} %copy.2753), channel_id=1, source_target_pairs={{0,8},{8,16},{16,24},{24,0},{1,9},{9,17},{17,25},{25,1},{2,10},{10... | collective-permute-start | bytes 1544 | tf_op jit(solution)/shard_map/ppermute | solution.py:24
  611.1 68.2 %collective-permute-start.46 = (f32[2,16,1]{2,1,0:T(8,128)S(1)}, f32[2,16,1]{2,1,0:T(8,128)S(1)}, u32[]{:S(2)}, u32[]{:S(2)}) collective-permute-start(f32[2,16,1]{2,1,0:T(8,128)S(1)} %get-tuple-element.190), channel_id=1, source_target_pairs={{1,0},{2,1},{3,2},{4,3},{5,4},{6,5},{7,6},{0,7},{9,8},{10,9},{11,1... | collective-permute-start | bytes 392 | tf_op jit(solution)/shard_map/ppermute | solution.py:26
  616.1 63.3 %collective-permute-start.47 = (f32[2,16,1]{2,1,0:T(8,128)S(1)}, f32[2,16,1]{2,1,0:T(8,128)S(1)}, u32[]{:S(2)}, u32[]{:S(2)}) collective-permute-start(f32[2,16,1]{2,1,0:T(8,128)S(1)} %get-tuple-element.191), channel_id=1, source_target_pairs={{0,1},{1,2},{2,3},{3,4},{4,5},{5,6},{6,7},{7,0},{8,9},{9,10},{10,1... | collective-permute-start | bytes 392 | tf_op jit(solution)/shard_map/ppermute | solution.py:24
  647.8 31.7 %collective-permute-start.45 = (f32[2,1,64]{2,1,0:T(1,128)S(1)}, f32[2,1,64]{2,1,0:T(1,128)S(1)}, u32[]{:S(2)}, u32[]{:S(2)}) collective-permute-start(f32[2,1,64]{2,1,0:T(1,128)S(1)} %copy.2779), channel_id=1, source_target_pairs={{0,8},{8,16},{16,24},{24,0},{1,9},{9,17},{17,25},{25,1},{2,10},{10... | collective-permute-start | bytes 1544 | tf_op jit(solution)/shard_map/ppermute | solution.py:24
  718.1 8.4 collective-permute-start.50
  888.1 8.4 collective-permute-start.56
  945.1 65.0 %collective-permute-start.66 = (f32[2,16,1]{2,1,0:T(8,128)S(1)}, f32[2,16,1]{2,1,0:T(8,128)S(1)}, u32[]{:S(2)}, u32[]{:S(2)}) collective-permute-start(f32[2,16,1]{2,1,0:T(8,128)S(1)} %get-tuple-element.184), channel_id=1, source_target_pairs={{1,0},{2,1},{3,2},{4,3},{5,4},{6,5},{7,6},{0,7},{9,8},{10,9},{11,1... | collective-permute-start | bytes 392 | tf_op jit(solution)/shard_map/ppermute | solution.py:26
  948.0 62.1 %collective-permute-start.67 = (f32[2,16,1]{2,1,0:T(8,128)S(1)}, f32[2,16,1]{2,1,0:T(8,128)S(1)}, u32[]{:S(2)}, u32[]{:S(2)}) collective-permute-start(f32[2,16,1]{2,1,0:T(8,128)S(1)} %get-tuple-element.185), channel_id=1, source_target_pairs={{0,1},{1,2},{2,3},{3,4},{4,5},{5,6},{6,7},{7,0},{8,9},{9,10},{10,1... | collective-permute-start | bytes 392 | tf_op jit(solution)/shard_map/ppermute | solution.py:24
  978.6 31.6 %collective-permute-start.65 = (f32[2,1,64]{2,1,0:T(1,128)S(1)}, f32[2,1,64]{2,1,0:T(1,128)S(1)}, u32[]{:S(2)}, u32[]{:S(2)}) collective-permute-start(f32[2,1,64]{2,1,0:T(1,128)S(1)} %copy.2803), channel_id=1, source_target_pairs={{0,8},{8,16},{16,24},{24,0},{1,9},{9,17},{17,25},{25,1},{2,10},{10... | collective-permute-start | bytes 1544 | tf_op jit(solution)/shard_map/ppermute | solution.py:24
  1059.7 67.9 %collective-permute-start.76 = (f32[2,16,1]{2,1,0:T(8,128)S(1)}, f32[2,16,1]{2,1,0:T(8,128)S(1)}, u32[]{:S(2)}, u32[]{:S(2)}) collective-permute-start(f32[2,16,1]{2,1,0:T(8,128)S(1)} %get-tuple-element.154), channel_id=1, source_target_pairs={{1,0},{2,1},{3,2},{4,3},{5,4},{6,5},{7,6},{0,7},{9,8},{10,9},{11,1... | collective-permute-start | bytes 392 | tf_op jit(solution)/shard_map/ppermute | solution.py:26
  1064.4 63.3 %collective-permute-start.77 = (f32[2,16,1]{2,1,0:T(8,128)S(1)}, f32[2,16,1]{2,1,0:T(8,128)S(1)}, u32[]{:S(2)}, u32[]{:S(2)}) collective-permute-start(f32[2,16,1]{2,1,0:T(8,128)S(1)} %get-tuple-element.155), channel_id=1, source_target_pairs={{0,1},{1,2},{2,3},{3,4},{4,5},{5,6},{6,7},{7,0},{8,9},{9,10},{10,1... | collective-permute-start | bytes 392 | tf_op jit(solution)/shard_map/ppermute | solution.py:24
  1096.0 31.6 %collective-permute-start.75 = (f32[2,1,64]{2,1,0:T(1,128)S(1)}, f32[2,1,64]{2,1,0:T(1,128)S(1)}, u32[]{:S(2)}, u32[]{:S(2)}) collective-permute-start(f32[2,1,64]{2,1,0:T(1,128)S(1)} %copy.2829), channel_id=1, source_target_pairs={{0,8},{8,16},{16,24},{24,0},{1,9},{9,17},{17,25},{25,1},{2,10},{10... | collective-permute-start | bytes 1544 | tf_op jit(solution)/shard_map/ppermute | solution.py:24
  1308.4 65.1 %collective-permute-start.92 = (f32[2,16,1]{2,1,0:T(8,128)S(1)}, f32[2,16,1]{2,1,0:T(8,128)S(1)}, u32[]{:S(2)}, u32[]{:S(2)}) collective-permute-start(f32[2,16,1]{2,1,0:T(8,128)S(1)} %get-tuple-element.148), channel_id=1, source_target_pairs={{1,0},{2,1},{3,2},{4,3},{5,4},{6,5},{7,6},{0,7},{9,8},{10,9},{11,1... | collective-permute-start | bytes 392 | tf_op jit(solution)/shard_map/ppermute | solution.py:26
  1311.4 62.2 %collective-permute-start.93 = (f32[2,16,1]{2,1,0:T(8,128)S(1)}, f32[2,16,1]{2,1,0:T(8,128)S(1)}, u32[]{:S(2)}, u32[]{:S(2)}) collective-permute-start(f32[2,16,1]{2,1,0:T(8,128)S(1)} %get-tuple-element.149), channel_id=1, source_target_pairs={{0,1},{1,2},{2,3},{3,4},{4,5},{5,6},{6,7},{7,0},{8,9},{9,10},{10,1... | collective-permute-start | bytes 392 | tf_op jit(solution)/shard_map/ppermute | solution.py:24
  1342.0 31.5 %collective-permute-start.91 = (f32[2,1,64]{2,1,0:T(1,128)S(1)}, f32[2,1,64]{2,1,0:T(1,128)S(1)}, u32[]{:S(2)}, u32[]{:S(2)}) collective-permute-start(f32[2,1,64]{2,1,0:T(1,128)S(1)} %copy.2849), channel_id=1, source_target_pairs={{0,8},{8,16},{16,24},{24,0},{1,9},{9,17},{17,25},{25,1},{2,10},{10... | collective-permute-start | bytes 1544 | tf_op jit(solution)/shard_map/ppermute | solution.py:24
  1423.0 68.1 %collective-permute-start.102 = (f32[2,16,1]{2,1,0:T(8,128)S(1)}, f32[2,16,1]{2,1,0:T(8,128)S(1)}, u32[]{:S(2)}, u32[]{:S(2)}) collective-permute-start(f32[2,16,1]{2,1,0:T(8,128)S(1)} %get-tuple-element.118), channel_id=1, source_target_pairs={{1,0},{2,1},{3,2},{4,3},{5,4},{6,5},{7,6},{0,7},{9,8},{10,9},{11,1... | collective-permute-start | bytes 392 | tf_op jit(solution)/shard_map/ppermute | solution.py:26
  1427.8 63.3 %collective-permute-start.103 = (f32[2,16,1]{2,1,0:T(8,128)S(1)}, f32[2,16,1]{2,1,0:T(8,128)S(1)}, u32[]{:S(2)}, u32[]{:S(2)}) collective-permute-start(f32[2,16,1]{2,1,0:T(8,128)S(1)} %get-tuple-element.119), channel_id=1, source_target_pairs={{0,1},{1,2},{2,3},{3,4},{4,5},{5,6},{6,7},{7,0},{8,9},{9,10},{10,1... | collective-permute-start | bytes 392 | tf_op jit(solution)/shard_map/ppermute | solution.py:24
  1459.3 31.8 %collective-permute-start.101 = (f32[2,1,64]{2,1,0:T(1,128)S(1)}, f32[2,1,64]{2,1,0:T(1,128)S(1)}, u32[]{:S(2)}, u32[]{:S(2)}) collective-permute-start(f32[2,1,64]{2,1,0:T(1,128)S(1)} %copy.2875), channel_id=1, source_target_pairs={{0,8},{8,16},{16,24},{24,0},{1,9},{9,17},{17,25},{25,1},{2,10},{10... | collective-permute-start | bytes 1544 | tf_op jit(solution)/shard_map/ppermute | solution.py:24
  (82 other events, 645.7 us)
where the time goes:
time: 1680 us; the launch traced here: 1670 us
  blocking collectives  1370 us (82%)
  starting transfers between devices  124 us (7%)
  local copies, waits for them, and re-layouts  83.3 us (5%)
  waiting for transfers between devices  56.8 us (3%)
    all_gather x22, blocking collectives, operate(): lax.all_gather(field[:, 0, :], 'gx', axis=1, tiled=True)  510 us
    all_gather x22, blocking collectives, operate(): lax.all_gather(field[:, -1, :], 'gx', axis=1, tiled=True)  487 us
    psum x6, blocking collectives, total_inner(): return lax.psum(jnp.sum(first_field * second_field), ('gy', 'gx'))  252 us
    all_gather x4, blocking collectives, coarsest(): gathered = lax.all_gather(residual, 'gx', axis=2, tiled=True)  123 us
    ppermute x56, starting transfers between devices, padded(): lax.ppermute(head, axis, [((i + 1) % count, i) for i in range(count)])  116 us
    ppermute x56, waiting for transfers between devices, padded(): lax.ppermute(tail, axis, [(i, (i + 1) % count) for i in range(count)])  43.9 us
  transfers between devices with their start and end apart: 112, of which 46 were waited for; matrix products, arithmetic and copies ran while one was open for 4% of the time, Pallas kernels for 0%

commit v1 on v0

--- a/solution.py
+++ b/solution.py
@@ -12,6 +12,27 @@
 VERTICAL = 1.0
 REACTION = 0.5
 ADVECTION = 0.5
+
+
+def gather_around(x, axis, dim):
+    length, index, rows = (lax.axis_size(axis), lax.axis_index(axis), x.shape[dim])
+    right = [(i, (i + 1) % length) for i in range(length)]
+    behind = [(i, (i - 1) % length) for i in range(length)]
+    filled = jnp.zeros((*x.shape[:dim], length * rows, *x.shape[dim + 1 :]), x.dtype)
+    filled = lax.dynamic_update_slice_in_dim(filled, x, index * rows, axis=dim)
+    from_left = from_right = x
+    half = length // 2
+    for step in range(1, half + 1):
+        from_left = lax.ppermute(from_left, axis, right)
+        filled = lax.dynamic_update_slice_in_dim(
+            filled, from_left, (index - step) % length * rows, axis=dim
+        )
+        if step < length - half:
+            from_right = lax.ppermute(from_right, axis, behind)
+            filled = lax.dynamic_update_slice_in_dim(
+                filled, from_right, (index + step) % length * rows, axis=dim
+            )
+    return filled
 
 
 def padded(cells, sides, width):
@@ -58,7 +79,7 @@
     columns = field.shape[2]
     margins = padded(field, (("gx", 2),), 1)
     bottom_full, upper_full = (
-        lax.all_gather(field[:, 0, :], "gx", axis=1, tiled=True),
+        gather_around(field[:, 0, :], "gx", 1),
         lax.all_gather(field[:, -1, :], "gx", axis=1, tiled=True),
     )
     right_field = margins[:, :, 2:]

time: 1680 us -> 1620 us (0.964)
  blocking collectives: 1370 us -> 954 us
  waiting for transfers between devices: 56.8 us -> 235 us
  starting transfers between devices: 124 us -> 296 us
    all_gather x22 -> x0, blocking collectives: 510 us -> none  [operate(): lax.all_gather(field[:, 0, :], 'gx', axis=1, tiled=True)]
    ppermute x0 -> x154, starting transfers between devices: none -> 206 us  [the longest x66 193 us: gather_around(): from_right = lax.ppermute(from_right, axis, behind)]
    ppermute x0 -> x154, waiting for transfers between devices: none -> 178 us  [the longest x88 177 us: gather_around(): from_left = lax.ppermute(from_left, axis, right)]
    all_gather x22, blocking collectives: 487 us -> 540 us  [operate(): lax.all_gather(field[:, -1, :], 'gx', axis=1, tiled=True)]
    ppermute x56, starting transfers between devices: 116 us -> 66.6 us  [padded(): lax.ppermute(head, axis, [((i + 1) % count, i) for i in range(count)])]
    psum x6, blocking collectives: 252 us -> 272 us  [total_inner(): return lax.psum(jnp.sum(first_field * second_field), ('gy', 'gx'))]
    all_gather x4, blocking collectives: 123 us -> 142 us  [coarsest(): gathered = lax.all_gather(residual, 'gx', axis=2, tiled=True)]
  transfers between devices with their start and end apart: 112 -> 266, of which waited for: 46 -> 104; matrix products, arithmetic and copies ran while one was open for 4% -> 4% of each run, Pallas kernels for 0% -> 0%
where the time goes in v1:
time: 1620 us; the launch traced here: 1610 us
  blocking collectives  954 us (59%)
  starting transfers between devices  296 us (18%)
  waiting for transfers between devices  235 us (15%)
  local copies, waits for them, and re-layouts  94.4 us (6%)
  between operations  19.1 us (1%)
    all_gather x22, blocking collectives, operate(): lax.all_gather(field[:, -1, :], 'gx', axis=1, tiled=True)  540 us
    psum x6, blocking collectives, total_inner(): return lax.psum(jnp.sum(first_field * second_field), ('gy', 'gx'))  272 us
    ppermute x66, starting transfers between devices, gather_around(): from_right = lax.ppermute(from_right, axis, behind)  193 us
    ppermute x88, waiting for transfers between devices, gather_around(): from_left = lax.ppermute(from_left, axis, right)  177 us
    all_gather x4, blocking collectives, coarsest(): gathered = lax.all_gather(residual, 'gx', axis=2, tiled=True)  142 us
    ppermute x56, starting transfers between devices, padded(): lax.ppermute(head, axis, [((i + 1) % count, i) for i in range(count)])  66.6 us
  transfers between devices with their start and end apart: 266, of which 104 were waited for; matrix products, arithmetic and copies ran while one was open for 4% of the time, Pallas kernels for 0%

profile of v1, /device:TPU:12, one launch (start us, length us, event | category | flops | bytes accessed | tf_op | source)
XLA Modules:
  0.0 1613.9 jit_solution(13143487693438751650)
XLA Ops:
  6.8 30.5 %all-gather = f32[2,1,1024]{0,2,1:T(8,128)S(1)} all-gather(f32[2,1,128]{0,2,1:T(8,128)S(1)} %copy.3694), channel_id=2, replica_groups=mesh['gy'=4,'gx'=8] {'gx'}, dimensions={2}, use_global_device_ids=true | all-gather | bytes 9216 | tf_op jit(solution)/shard_map/all_gather | solution.py:83
  76.6 20.9 %all-gather.1 = f32[2,1,1024]{2,1,0:T(1,128)S(1)} all-gather(f32[2,1,128]{2,1,0:T(1,128)S(1)} %get-tuple-element.105), channel_id=3, replica_groups=mesh['gy'=4,'gx'=8] {'gx'}, dimensions={2}, use_global_device_ids=true | all-gather | bytes 9216 | tf_op jit(solution)/shard_map/all_gather | solution.py:83
  125.4 35.3 %all-gather.2 = f32[2,1,512]{0,1,2:T(1,128)S(1)} all-gather(f32[2,1,64]{0,1,2:T(1,128)S(1)} %copy.3345), channel_id=4, replica_groups=mesh['gy'=4,'gx'=8] {'gx'}, dimensions={2}, use_global_device_ids=true | all-gather | bytes 4608 | tf_op jit(solution)/shard_map/all_gather | solution.py:83
  181.7 35.5 %all_gather.81 = f32[2,8,256]{1,0,2:T(2,128)S(1)} all-gather(f32[2,8,32]{1,0,2:T(2,128)S(1)} %copy.3348), channel_id=1, replica_groups=mesh['gy'=4,'gx'=8] {'gx'}, dimensions={2}, use_global_device_ids=true | all-gather | bytes 18432 | tf_op jit(solution)/shard_map/all_gather | solution.py:103
  236.6 32.6 %all-gather.3 = f32[2,1,512]{0,1,2:T(1,128)S(1)} all-gather(f32[2,1,64]{0,1,2:T(1,128)S(1)} %copy.3373), channel_id=5, replica_groups=mesh['gy'=4,'gx'=8] {'gx'}, dimensions={2}, use_global_device_ids=true | all-gather | bytes 4608 | tf_op jit(solution)/shard_map/all_gather | solution.py:83
  294.7 20.9 %all-gather.4 = f32[2,1,1024]{2,1,0:T(1,128)S(1)} all-gather(f32[2,1,128]{2,1,0:T(1,128)S(1)} %get-tuple-element.99), channel_id=6, replica_groups=mesh['gy'=4,'gx'=8] {'gx'}, dimensions={2}, use_global_device_ids=true | all-gather | bytes 9216 | tf_op jit(solution)/shard_map/all_gather | solution.py:83
  341.1 20.8 %all-gather.5 = f32[2,1,1024]{2,1,0:T(1,128)S(1)} all-gather(f32[2,1,128]{2,1,0:T(1,128)S(1)} %get-tuple-element.91), channel_id=7, replica_groups=mesh['gy'=4,'gx'=8] {'gx'}, dimensions={2}, use_global_device_ids=true | all-gather | bytes 9216 | tf_op jit(solution)/shard_map/all_gather | solution.py:83
  384.7 45.5 %all-reduce.1 = (f32[]{:T(128)}, f32[]{:T(128)}) all-reduce(f32[]{:T(128)} %get-tuple-element.11, f32[]{:T(128)} %get-tuple-element.10), channel_id=1, replica_groups=mesh['gy'=4,'gx'=8] {'gy','gx'}, use_global_device_ids=true, to_apply=%region_3.7 | all-reduce | flops 2 | bytes 16 | tf_op jit(solution)/shard_map/psum | solution.py:133
  434.7 14.0 all-gather.6
  476.6 35.2 %all-gather.7 = f32[2,1,512]{0,1,2:T(1,128)S(1)} all-gather(f32[2,1,64]{0,1,2:T(1,128)S(1)} %copy.3416), channel_id=9, replica_groups=mesh['gy'=4,'gx'=8] {'gx'}, dimensions={2}, use_global_device_ids=true | all-gather | bytes 4608 | tf_op jit(solution)/shard_map/all_gather | solution.py:83
  532.8 35.7 %all_gather.87 = f32[2,8,256]{1,0,2:T(2,128)S(1)} all-gather(f32[2,8,32]{1,0,2:T(2,128)S(1)} %copy.3419), channel_id=1, replica_groups=mesh['gy'=4,'gx'=8] {'gx'}, dimensions={2}, use_global_device_ids=true | all-gather | bytes 18432 | tf_op jit(solution)/shard_map/all_gather | solution.py:103
  588.3 32.6 %all-gather.8 = f32[2,1,512]{0,1,2:T(1,128)S(1)} all-gather(f32[2,1,64]{0,1,2:T(1,128)S(1)} %copy.3444), channel_id=10, replica_groups=mesh['gy'=4,'gx'=8] {'gx'}, dimensions={2}, use_global_device_ids=true | all-gather | bytes 4608 | tf_op jit(solution)/shard_map/all_gather | solution.py:83
  646.3 20.9 %all-gather.9 = f32[2,1,1024]{2,1,0:T(1,128)S(1)} all-gather(f32[2,1,128]{2,1,0:T(1,128)S(1)} %get-tuple-element.79), channel_id=11, replica_groups=mesh['gy'=4,'gx'=8] {'gx'}, dimensions={2}, use_global_device_ids=true | all-gather | bytes 9216 | tf_op jit(solution)/shard_map/all_gather | solution.py:83
  690.1 45.5 %psum.58 = f32[]{:T(128)} all-reduce(f32[]{:T(128)} %get-tuple-element.23), channel_id=1, replica_groups=mesh['gy'=4,'gx'=8] {'gy','gx'}, use_global_device_ids=true, to_apply=%region_9.13 | all-reduce | flops 1 | bytes 8 | tf_op jit(solution)/shard_map/psum | solution.py:133
  740.0 14.0 all-gather.10
  776.8 45.1 %psum.59 = f32[]{:T(128)} all-reduce(f32[]{:T(128)} %fusion.65), channel_id=1, replica_groups=mesh['gy'=4,'gx'=8] {'gy','gx'}, use_global_device_ids=true, to_apply=%region_11.15 | all-reduce | flops 1 | bytes 8 | tf_op jit(solution)/shard_map/psum | solution.py:133
  826.5 14.3 all-gather.11
  865.9 20.9 %all-gather.12 = f32[2,1,1024]{2,1,0:T(1,128)S(1)} all-gather(f32[2,1,128]{2,1,0:T(1,128)S(1)} %get-tuple-element.63), channel_id=14, replica_groups=mesh['gy'=4,'gx'=8] {'gx'}, dimensions={2}, use_global_device_ids=true | all-gather | bytes 9216 | tf_op jit(solution)/shard_map/all_gather | solution.py:83
  914.9 35.2 %all-gather.13 = f32[2,1,512]{0,1,2:T(1,128)S(1)} all-gather(f32[2,1,64]{0,1,2:T(1,128)S(1)} %copy.3498), channel_id=15, replica_groups=mesh['gy'=4,'gx'=8] {'gx'}, dimensions={2}, use_global_device_ids=true | all-gather | bytes 4608 | tf_op jit(solution)/shard_map/all_gather | solution.py:83
  971.1 35.5 %all_gather.94 = f32[2,8,256]{1,0,2:T(2,128)S(1)} all-gather(f32[2,8,32]{1,0,2:T(2,128)S(1)} %copy.3501), channel_id=1, replica_groups=mesh['gy'=4,'gx'=8] {'gx'}, dimensions={2}, use_global_device_ids=true | all-gather | bytes 18432 | tf_op jit(solution)/shard_map/all_gather | solution.py:103
  1026.0 32.6 %all-gather.14 = f32[2,1,512]{0,1,2:T(1,128)S(1)} all-gather(f32[2,1,64]{0,1,2:T(1,128)S(1)} %copy.3526), channel_id=16, replica_groups=mesh['gy'=4,'gx'=8] {'gx'}, dimensions={2}, use_global_device_ids=true | all-gather | bytes 4608 | tf_op jit(solution)/shard_map/all_gather | solution.py:83
  1084.0 20.9 %all-gather.15 = f32[2,1,1024]{2,1,0:T(1,128)S(1)} all-gather(f32[2,1,128]{2,1,0:T(1,128)S(1)} %get-tuple-element.57), channel_id=17, replica_groups=mesh['gy'=4,'gx'=8] {'gx'}, dimensions={2}, use_global_device_ids=true | all-gather | bytes 9216 | tf_op jit(solution)/shard_map/all_gather | solution.py:83
  1130.4 20.8 %all-gather.16 = f32[2,1,1024]{2,1,0:T(1,128)S(1)} all-gather(f32[2,1,128]{2,1,0:T(1,128)S(1)} %get-tuple-element.49), channel_id=18, replica_groups=mesh['gy'=4,'gx'=8] {'gx'}, dimensions={2}, use_global_device_ids=true | all-gather | bytes 9216 | tf_op jit(solution)/shard_map/all_gather | solution.py:83
  1174.5 45.3 %all-reduce = (f32[]{:T(128)}, f32[]{:T(128)}) all-reduce(f32[]{:T(128)} %get-tuple-element.8, f32[]{:T(128)} %get-tuple-element.6), channel_id=1, replica_groups=mesh['gy'=4,'gx'=8] {'gy','gx'}, use_global_device_ids=true, to_apply=%region_15.19 | all-reduce | flops 2 | bytes 16 | tf_op jit(solution)/shard_map/psum | solution.py:133
  1224.3 14.1 all-gather.17
  1266.2 35.4 %all-gather.18 = f32[2,1,512]{0,1,2:T(1,128)S(1)} all-gather(f32[2,1,64]{0,1,2:T(1,128)S(1)} %copy.3569), channel_id=20, replica_groups=mesh['gy'=4,'gx'=8] {'gx'}, dimensions={2}, use_global_device_ids=true | all-gather | bytes 4608 | tf_op jit(solution)/shard_map/all_gather | solution.py:83
  1322.5 35.7 %all_gather.100 = f32[2,8,256]{1,0,2:T(2,128)S(1)} all-gather(f32[2,8,32]{1,0,2:T(2,128)S(1)} %copy.3572), channel_id=1, replica_groups=mesh['gy'=4,'gx'=8] {'gx'}, dimensions={2}, use_global_device_ids=true | all-gather | bytes 18432 | tf_op jit(solution)/shard_map/all_gather | solution.py:103
  1377.6 32.6 %all-gather.19 = f32[2,1,512]{0,1,2:T(1,128)S(1)} all-gather(f32[2,1,64]{0,1,2:T(1,128)S(1)} %copy.3597), channel_id=21, replica_groups=mesh['gy'=4,'gx'=8] {'gx'}, dimensions={2}, use_global_device_ids=true | all-gather | bytes 4608 | tf_op jit(solution)/shard_map/all_gather | solution.py:83
  1435.8 20.9 %all-gather.20 = f32[2,1,1024]{2,1,0:T(1,128)S(1)} all-gather(f32[2,1,128]{2,1,0:T(1,128)S(1)} %get-tuple-element.37), channel_id=22, replica_groups=mesh['gy'=4,'gx'=8] {'gx'}, dimensions={2}, use_global_device_ids=true | all-gather | bytes 9216 | tf_op jit(solution)/shard_map/all_gather | solution.py:83
  1479.6 45.5 %psum.62 = f32[]{:T(128)} all-reduce(f32[]{:T(128)} %get-tuple-element.16), channel_id=1, replica_groups=mesh['gy'=4,'gx'=8] {'gy','gx'}, use_global_device_ids=true, to_apply=%region_21.25 | all-reduce | flops 1 | bytes 8 | tf_op jit(solution)/shard_map/psum | solution.py:133
  1529.5 14.0 all-gather.21
  1566.3 45.1 %psum.63 = f32[]{:T(128)} all-reduce(f32[]{:T(128)} %fusion.14), channel_id=1, replica_groups=mesh['gy'=4,'gx'=8] {'gy','gx'}, use_global_device_ids=true, to_apply=%region_23.27 | all-reduce | flops 1 | bytes 8 | tf_op jit(solution)/shard_map/psum | solution.py:133
  (1392 shorter events, 640.7 us)
Async XLA Ops:
  0.9 52.3 %collective-permute-start.2 = (f32[2,128]{0,1:T(8,128)S(1)}, f32[2,128]{0,1:T(8,128)S(1)}, u32[]{:S(2)}, u32[]{:S(2)}) collective-permute-start(f32[2,128]{0,1:T(8,128)S(1)} %bitcast.349), channel_id=1, source_target_pairs={{0,1},{1,2},{2,3},{3,4},{4,5},{5,6},{6,7},{7,0},{8,9},{9,10},{10,1... | collective-permute-start | bytes 3080 | tf_op jit(solution)/shard_map/ppermute | solution.py:26
  2.4 50.9 %collective-permute-start.3 = (f32[2,128]{0,1:T(8,128)S(1)}, f32[2,128]{0,1:T(8,128)S(1)}, u32[]{:S(2)}, u32[]{:S(2)}) collective-permute-start(f32[2,128]{0,1:T(8,128)S(1)} %bitcast.350), channel_id=1, source_target_pairs={{0,7},{1,0},{2,1},{3,2},{4,3},{5,4},{6,5},{7,6},{8,15},{9,8},{10,9... | collective-permute-start | bytes 3080 | tf_op jit(solution)/shard_map/ppermute | solution.py:31
  38.0 33.0 %collective-permute-start.10 = (f32[2,1,128]{2,1,0:T(1,128)S(1)}, f32[2,1,128]{2,1,0:T(1,128)S(1)}, u32[]{:S(2)}, u32[]{:S(2)}) collective-permute-start(f32[2,1,128]{2,1,0:T(1,128)S(1)} %bitcast.430), channel_id=1, source_target_pairs={{0,8},{8,16},{16,24},{24,0},{1,9},{9,17},{17,25},{25,1},{2,10},{10... | collective-permute-start | bytes 3080 | tf_op jit(solution)/shard_map/ppermute | solution.py:45
  38.9 32.0 %collective-permute-start = (f32[2,32,1]{2,1,0:T(8,128)S(1)}, f32[2,32,1]{2,1,0:T(8,128)S(1)}, u32[]{:S(2)}, u32[]{:S(2)}) collective-permute-start(f32[2,32,1]{2,1,0:T(8,128)S(1)} %get-tuple-element.108), channel_id=1, source_target_pairs={{1,0},{2,1},{3,2},{4,3},{5,4},{6,5},{7,6},{0,7},{9,8},{10,9},{11,1... | collective-permute-start | bytes 776 | tf_op jit(solution)/shard_map/ppermute | solution.py:47
  40.6 30.4 %collective-permute-start.1 = (f32[2,32,1]{2,1,0:T(8,128)S(1)}, f32[2,32,1]{2,1,0:T(8,128)S(1)}, u32[]{:S(2)}, u32[]{:S(2)}) collective-permute-start(f32[2,32,1]{2,1,0:T(8,128)S(1)} %get-tuple-element.109), channel_id=1, source_target_pairs={{0,1},{1,2},{2,3},{3,4},{4,5},{5,6},{6,7},{7,0},{8,9},{9,10},{10,1... | collective-permute-start | bytes 776 | tf_op jit(solution)/shard_map/ppermute | solution.py:45
  72.5 30.9 %collective-permute-start.11 = (f32[2,128]{1,0:T(2,128)S(1)}, f32[2,128]{1,0:T(2,128)S(1)}, u32[]{:S(2)}, u32[]{:S(2)}) collective-permute-start(f32[2,128]{1,0:T(2,128)S(1)} %bitcast.390), channel_id=1, source_target_pairs={{0,1},{1,2},{2,3},{3,4},{4,5},{5,6},{6,7},{7,0},{8,9},{9,10},{10,1... | collective-permute-start | bytes 3080 | tf_op jit(solution)/shard_map/ppermute | solution.py:26
  72.5 31.2 %collective-permute-start.12 = (f32[2,128]{1,0:T(2,128)S(1)}, f32[2,128]{1,0:T(2,128)S(1)}, u32[]{:S(2)}, u32[]{:S(2)}) collective-permute-start(f32[2,128]{1,0:T(2,128)S(1)} %bitcast.391), channel_id=1, source_target_pairs={{0,7},{1,0},{2,1},{3,2},{4,3},{5,4},{6,5},{7,6},{8,15},{9,8},{10,9... | collective-permute-start | bytes 3080 | tf_op jit(solution)/shard_map/ppermute | solution.py:31
  122.3 41.3 %collective-permute-start.22 = (f32[2,64]{0,1:T(8,128)S(1)}, f32[2,64]{0,1:T(8,128)S(1)}, u32[]{:S(2)}, u32[]{:S(2)}) collective-permute-start(f32[2,64]{0,1:T(8,128)S(1)} %copy.3340), channel_id=1, source_target_pairs={{0,1},{1,2},{2,3},{3,4},{4,5},{5,6},{6,7},{7,0},{8,9},{9,10},{10,1... | collective-permute-start | bytes 1544 | tf_op jit(solution)/shard_map/ppermute | solution.py:26
  122.3 41.3 %collective-permute-start.23 = (f32[2,64]{0,1:T(8,128)S(1)}, f32[2,64]{0,1:T(8,128)S(1)}, u32[]{:S(2)}, u32[]{:S(2)}) collective-permute-start(f32[2,64]{0,1:T(8,128)S(1)} %copy.3340), channel_id=1, source_target_pairs={{0,7},{1,0},{2,1},{3,2},{4,3},{5,4},{6,5},{7,6},{8,15},{9,8},{10,9... | collective-permute-start | bytes 1544 | tf_op jit(solution)/shard_map/ppermute | solution.py:31
  233.5 38.6 %collective-permute-start.39 = (f32[2,64]{0,1:T(8,128)S(1)}, f32[2,64]{0,1:T(8,128)S(1)}, u32[]{:S(2)}, u32[]{:S(2)}) collective-permute-start(f32[2,64]{0,1:T(8,128)S(1)} %copy.3368), channel_id=1, source_target_pairs={{0,1},{1,2},{2,3},{3,4},{4,5},{5,6},{6,7},{7,0},{8,9},{9,10},{10,1... | collective-permute-start | bytes 1544 | tf_op jit(solution)/shard_map/ppermute | solution.py:26
  233.5 38.8 %collective-permute-start.40 = (f32[2,64]{0,1:T(8,128)S(1)}, f32[2,64]{0,1:T(8,128)S(1)}, u32[]{:S(2)}, u32[]{:S(2)}) collective-permute-start(f32[2,64]{0,1:T(8,128)S(1)} %copy.3368), channel_id=1, source_target_pairs={{0,7},{1,0},{2,1},{3,2},{4,3},{5,4},{6,5},{7,6},{8,15},{9,8},{10,9... | collective-permute-start | bytes 1544 | tf_op jit(solution)/shard_map/ppermute | solution.py:31
  289.8 31.7 %collective-permute-start.50 = (f32[2,128]{1,0:T(2,128)S(1)}, f32[2,128]{1,0:T(2,128)S(1)}, u32[]{:S(2)}, u32[]{:S(2)}) collective-permute-start(f32[2,128]{1,0:T(2,128)S(1)} %bitcast.393), channel_id=1, source_target_pairs={{0,1},{1,2},{2,3},{3,4},{4,5},{5,6},{6,7},{7,0},{8,9},{9,10},{10,1... | collective-permute-start | bytes 3080 | tf_op jit(solution)/shard_map/ppermute | solution.py:26
  289.9 32.0 %collective-permute-start.51 = (f32[2,128]{1,0:T(2,128)S(1)}, f32[2,128]{1,0:T(2,128)S(1)}, u32[]{:S(2)}, u32[]{:S(2)}) collective-permute-start(f32[2,128]{1,0:T(2,128)S(1)} %bitcast.394), channel_id=1, source_target_pairs={{0,7},{1,0},{2,1},{3,2},{4,3},{5,4},{6,5},{7,6},{8,15},{9,8},{10,9... | collective-permute-start | bytes 3080 | tf_op jit(solution)/shard_map/ppermute | solution.py:31
  473.5 41.2 %collective-permute-start.83 = (f32[2,64]{0,1:T(8,128)S(1)}, f32[2,64]{0,1:T(8,128)S(1)}, u32[]{:S(2)}, u32[]{:S(2)}) collective-permute-start(f32[2,64]{0,1:T(8,128)S(1)} %copy.3411), channel_id=1, source_target_pairs={{0,1},{1,2},{2,3},{3,4},{4,5},{5,6},{6,7},{7,0},{8,9},{9,10},{10,1... | collective-permute-start | bytes 1544 | tf_op jit(solution)/shard_map/ppermute | solution.py:26
  473.5 41.2 %collective-permute-start.84 = (f32[2,64]{0,1:T(8,128)S(1)}, f32[2,64]{0,1:T(8,128)S(1)}, u32[]{:S(2)}, u32[]{:S(2)}) collective-permute-start(f32[2,64]{0,1:T(8,128)S(1)} %copy.3411), channel_id=1, source_target_pairs={{0,7},{1,0},{2,1},{3,2},{4,3},{5,4},{6,5},{7,6},{8,15},{9,8},{10,9... | collective-permute-start | bytes 1544 | tf_op jit(solution)/shard_map/ppermute | solution.py:31
  585.2 38.6 %collective-permute-start.100 = (f32[2,64]{0,1:T(8,128)S(1)}, f32[2,64]{0,1:T(8,128)S(1)}, u32[]{:S(2)}, u32[]{:S(2)}) collective-permute-start(f32[2,64]{0,1:T(8,128)S(1)} %copy.3439), channel_id=1, source_target_pairs={{0,1},{1,2},{2,3},{3,4},{4,5},{5,6},{6,7},{7,0},{8,9},{9,10},{10,1... | collective-permute-start | bytes 1544 | tf_op jit(solution)/shard_map/ppermute | solution.py:26
  585.2 38.6 %collective-permute-start.101 = (f32[2,64]{0,1:T(8,128)S(1)}, f32[2,64]{0,1:T(8,128)S(1)}, u32[]{:S(2)}, u32[]{:S(2)}) collective-permute-start(f32[2,64]{0,1:T(8,128)S(1)} %copy.3439), channel_id=1, source_target_pairs={{0,7},{1,0},{2,1},{3,2},{4,3},{5,4},{6,5},{7,6},{8,15},{9,8},{10,9... | collective-permute-start | bytes 1544 | tf_op jit(solution)/shard_map/ppermute | solution.py:31
  641.4 31.6 %collective-permute-start.111 = (f32[2,128]{1,0:T(2,128)S(1)}, f32[2,128]{1,0:T(2,128)S(1)}, u32[]{:S(2)}, u32[]{:S(2)}) collective-permute-start(f32[2,128]{1,0:T(2,128)S(1)} %bitcast.402), channel_id=1, source_target_pairs={{0,1},{1,2},{2,3},{3,4},{4,5},{5,6},{6,7},{7,0},{8,9},{9,10},{10,1... | collective-permute-start | bytes 3080 | tf_op jit(solution)/shard_map/ppermute | solution.py:26
  641.5 32.0 %collective-permute-start.112 = (f32[2,128]{1,0:T(2,128)S(1)}, f32[2,128]{1,0:T(2,128)S(1)}, u32[]{:S(2)}, u32[]{:S(2)}) collective-permute-start(f32[2,128]{1,0:T(2,128)S(1)} %bitcast.403), channel_id=1, source_target_pairs={{0,7},{1,0},{2,1},{3,2},{4,3},{5,4},{6,5},{7,6},{8,15},{9,8},{10,9... | collective-permute-start | bytes 3080 | tf_op jit(solution)/shard_map/ppermute | solution.py:31
  862.9 30.4 %collective-permute-start.145 = (f32[2,128]{1,0:T(2,128)S(1)}, f32[2,128]{1,0:T(2,128)S(1)}, u32[]{:S(2)}, u32[]{:S(2)}) collective-permute-start(f32[2,128]{1,0:T(2,128)S(1)} %bitcast.409), channel_id=1, source_target_pairs={{0,7},{1,0},{2,1},{3,2},{4,3},{5,4},{6,5},{7,6},{8,15},{9,8},{10,9... | collective-permute-start | bytes 3080 | tf_op jit(solution)/shard_map/ppermute | solution.py:31
  911.8 41.2 %collective-permute-start.155 = (f32[2,64]{0,1:T(8,128)S(1)}, f32[2,64]{0,1:T(8,128)S(1)}, u32[]{:S(2)}, u32[]{:S(2)}) collective-permute-start(f32[2,64]{0,1:T(8,128)S(1)} %copy.3493), channel_id=1, source_target_pairs={{0,1},{1,2},{2,3},{3,4},{4,5},{5,6},{6,7},{7,0},{8,9},{9,10},{10,1... | collective-permute-start | bytes 1544 | tf_op jit(solution)/shard_map/ppermute | solution.py:26
  911.8 41.2 %collective-permute-start.156 = (f32[2,64]{0,1:T(8,128)S(1)}, f32[2,64]{0,1:T(8,128)S(1)}, u32[]{:S(2)}, u32[]{:S(2)}) collective-permute-start(f32[2,64]{0,1:T(8,128)S(1)} %copy.3493), channel_id=1, source_target_pairs={{0,7},{1,0},{2,1},{3,2},{4,3},{5,4},{6,5},{7,6},{8,15},{9,8},{10,9... | collective-permute-start | bytes 1544 | tf_op jit(solution)/shard_map/ppermute | solution.py:31
  1022.9 38.6 %collective-permute-start.172 = (f32[2,64]{0,1:T(8,128)S(1)}, f32[2,64]{0,1:T(8,128)S(1)}, u32[]{:S(2)}, u32[]{:S(2)}) collective-permute-start(f32[2,64]{0,1:T(8,128)S(1)} %copy.3521), channel_id=1, source_target_pairs={{0,1},{1,2},{2,3},{3,4},{4,5},{5,6},{6,7},{7,0},{8,9},{9,10},{10,1... | collective-permute-start | bytes 1544 | tf_op jit(solution)/shard_map/ppermute | solution.py:26
  1022.9 38.6 %collective-permute-start.173 = (f32[2,64]{0,1:T(8,128)S(1)}, f32[2,64]{0,1:T(8,128)S(1)}, u32[]{:S(2)}, u32[]{:S(2)}) collective-permute-start(f32[2,64]{0,1:T(8,128)S(1)} %copy.3521), channel_id=1, source_target_pairs={{0,7},{1,0},{2,1},{3,2},{4,3},{5,4},{6,5},{7,6},{8,15},{9,8},{10,9... | collective-permute-start | bytes 1544 | tf_op jit(solution)/shard_map/ppermute | solution.py:31
  1079.1 31.6 %collective-permute-start.183 = (f32[2,128]{1,0:T(2,128)S(1)}, f32[2,128]{1,0:T(2,128)S(1)}, u32[]{:S(2)}, u32[]{:S(2)}) collective-permute-start(f32[2,128]{1,0:T(2,128)S(1)} %bitcast.411), channel_id=1, source_target_pairs={{0,1},{1,2},{2,3},{3,4},{4,5},{5,6},{6,7},{7,0},{8,9},{9,10},{10,1... | collective-permute-start | bytes 3080 | tf_op jit(solution)/shard_map/ppermute | solution.py:26
  1079.2 32.0 %collective-permute-start.184 = (f32[2,128]{1,0:T(2,128)S(1)}, f32[2,128]{1,0:T(2,128)S(1)}, u32[]{:S(2)}, u32[]{:S(2)}) collective-permute-start(f32[2,128]{1,0:T(2,128)S(1)} %bitcast.412), channel_id=1, source_target_pairs={{0,7},{1,0},{2,1},{3,2},{4,3},{5,4},{6,5},{7,6},{8,15},{9,8},{10,9... | collective-permute-start | bytes 3080 | tf_op jit(solution)/shard_map/ppermute | solution.py:31
  1263.1 41.3 %collective-permute-start.216 = (f32[2,64]{0,1:T(8,128)S(1)}, f32[2,64]{0,1:T(8,128)S(1)}, u32[]{:S(2)}, u32[]{:S(2)}) collective-permute-start(f32[2,64]{0,1:T(8,128)S(1)} %copy.3564), channel_id=1, source_target_pairs={{0,1},{1,2},{2,3},{3,4},{4,5},{5,6},{6,7},{7,0},{8,9},{9,10},{10,1... | collective-permute-start | bytes 1544 | tf_op jit(solution)/shard_map/ppermute | solution.py:26
  1263.1 41.3 %collective-permute-start.217 = (f32[2,64]{0,1:T(8,128)S(1)}, f32[2,64]{0,1:T(8,128)S(1)}, u32[]{:S(2)}, u32[]{:S(2)}) collective-permute-start(f32[2,64]{0,1:T(8,128)S(1)} %copy.3564), channel_id=1, source_target_pairs={{0,7},{1,0},{2,1},{3,2},{4,3},{5,4},{6,5},{7,6},{8,15},{9,8},{10,9... | collective-permute-start | bytes 1544 | tf_op jit(solution)/shard_map/ppermute | solution.py:31
  1374.5 38.6 %collective-permute-start.233 = (f32[2,64]{0,1:T(8,128)S(1)}, f32[2,64]{0,1:T(8,128)S(1)}, u32[]{:S(2)}, u32[]{:S(2)}) collective-permute-start(f32[2,64]{0,1:T(8,128)S(1)} %copy.3592), channel_id=1, source_target_pairs={{0,1},{1,2},{2,3},{3,4},{4,5},{5,6},{6,7},{7,0},{8,9},{9,10},{10,1... | collective-permute-start | bytes 1544 | tf_op jit(solution)/shard_map/ppermute | solution.py:26
  1374.5 38.6 %collective-permute-start.234 = (f32[2,64]{0,1:T(8,128)S(1)}, f32[2,64]{0,1:T(8,128)S(1)}, u32[]{:S(2)}, u32[]{:S(2)}) collective-permute-start(f32[2,64]{0,1:T(8,128)S(1)} %copy.3592), channel_id=1, source_target_pairs={{0,7},{1,0},{2,1},{3,2},{4,3},{5,4},{6,5},{7,6},{8,15},{9,8},{10,9... | collective-permute-start | bytes 1544 | tf_op jit(solution)/shard_map/ppermute | solution.py:31
  1430.9 31.6 %collective-permute-start.244 = (f32[2,128]{1,0:T(2,128)S(1)}, f32[2,128]{1,0:T(2,128)S(1)}, u32[]{:S(2)}, u32[]{:S(2)}) collective-permute-start(f32[2,128]{1,0:T(2,128)S(1)} %bitcast.420), channel_id=1, source_target_pairs={{0,1},{1,2},{2,3},{3,4},{4,5},{5,6},{6,7},{7,0},{8,9},{9,10},{10,1... | collective-permute-start | bytes 3080 | tf_op jit(solution)/shard_map/ppermute | solution.py:26
  1431.0 32.0 %collective-permute-start.245 = (f32[2,128]{1,0:T(2,128)S(1)}, f32[2,128]{1,0:T(2,128)S(1)}, u32[]{:S(2)}, u32[]{:S(2)}) collective-permute-start(f32[2,128]{1,0:T(2,128)S(1)} %bitcast.421), channel_id=1, source_target_pairs={{0,7},{1,0},{2,1},{3,2},{4,3},{5,4},{6,5},{7,6},{8,15},{9,8},{10,9... | collective-permute-start | bytes 3080 | tf_op jit(solution)/shard_map/ppermute | solution.py:31
  (236 other events, 2274.5 us)
